TPU v7x, 32 devices: a whole 2x2x4 slice. The times are simulated.
32 devices in a mesh: lat: 8 (over z, y), lon: 4 (over x, core).
Axes of the slice: x: 2, y: 2, z: 4, core: 2. Of those that a mesh axis runs over, the one named last changes fastest.
Arguments:
- grid_field: float32 [384, 64, 512], P(None, 'lat', 'lon'), may hold values from -6 to 6
- disco_dlat: int32 [64, 16], P('lat'), may hold values from -2 to 2
- disco_dlon: int32 [64, 16], P('lat'), may hold values from -2 to 2
- disco_basis: int32 [64, 16], P('lat'), may hold values from 0 to 3
- disco_quad: float32 [64, 16], P('lat'), may hold values from 0.05 to 0.5
- disco_weight: bfloat16 [4, 384, 384], replicated, may hold values from -0.3125 to 0.3125
- norm_gain: float32 [384], replicated, may hold values from 0.1 to 1.9
- spectral_filter: float32 [384, 64], replicated, may hold values from -6 to 6
- mix_weight: bfloat16 [384, 384], replicated, may hold values from -0.3125 to 0.3125
Outputs:
- updated: float32 [384, 64, 512], P(None, 'lat', 'lon')
All inputs are finite; a program needn't handle non-finite values.
Results may differ from a plain program's by a relative error of at most 0.0044.
Values may be sent and summed in bfloat16 or wider, within the bound.
A program may use at most 64 MiB of HBM per device.

v0:
```python
import math
import jax
import jax.numpy as jnp
from jax import lax
from jax.sharding import PartitionSpec as P

M_DEV = 8
HALO = 2


def padded_2(cells, sides, width):
    for axis, dim in sides:
        count = lax.axis_size(axis)
        head = lax.slice_in_dim(cells, 0, width, axis=dim)
        tail = lax.slice_in_dim(cells, cells.shape[dim] - width, cells.shape[dim], axis=dim)
        cells = jnp.concatenate(
            [
                lax.ppermute(tail, axis, [(i, (i + 1) % count) for i in range(count)]),
                cells,
                lax.ppermute(head, axis, [((i + 1) % count, i) for i in range(count)]),
            ],
            axis=dim,
        )
    return cells


def legendre_table(first_order, local_orders, all_orders, degrees, nlat):
    lat_pos = jnp.arange(nlat, dtype=jnp.float32)
    colatitude = math.pi * (lat_pos + 0.5) / nlat
    cosine = jnp.cos(colatitude)
    sine = jnp.sin(colatitude)
    counters = jnp.arange(1, all_orders, dtype=jnp.float32)
    cumulative = jnp.concatenate(
        [
            jnp.zeros((1,), jnp.float32),
            jnp.cumsum(jnp.log((2.0 * counters - 1.0) / (2.0 * counters))),
        ]
    )
    log_product = lax.dynamic_slice_in_dim(cumulative, first_order, local_orders)
    orders = first_order + jnp.arange(local_orders, dtype=jnp.int32)
    order_real = orders.astype(jnp.float32)[:, None]
    log_seed = (
        0.5 * (jnp.log((2.0 * order_real + 1.0) / (4.0 * math.pi)) + log_product[:, None])
        + order_real * jnp.log(sine)[None, :]
    )
    rescale = jnp.clip(-log_seed, 0.0, 80.0)
    seed_value = jnp.exp(log_seed + rescale)
    undo = jnp.exp(-rescale)

    def advance(state_pair, degree):
        previous, before_last = state_pair
        degree_real = degree.astype(jnp.float32)
        factor_a = jnp.sqrt(
            jnp.maximum(4.0 * degree_real**2 - 1.0, 1.0)
            / jnp.maximum(degree_real**2 - order_real**2, 1.0)
        )
        factor_b = jnp.sqrt(
            jnp.maximum((degree_real - 1.0) ** 2 - order_real**2, 0.0)
            / jnp.maximum(4.0 * (degree_real - 1.0) ** 2 - 1.0, 1.0)
        )
        recurred = factor_a * (cosine[None, :] * previous - factor_b * before_last)
        current = jnp.where(
            degree == orders[:, None],
            seed_value,
            jnp.where(degree > orders[:, None], recurred, 0.0),
        )
        return ((current, previous), current * undo)

    empty = jnp.zeros((local_orders, nlat), jnp.float32)
    final_pair, table = lax.scan(
        advance, (empty, empty), jnp.arange(degrees, dtype=jnp.int32), unroll=8
    )
    return table


def disco_rows(padded, disco_dlat, disco_dlon, disco_basis, disco_quad, disco_weight, width):
    basis_count = disco_weight.shape[0]
    channels = padded.shape[0]
    zero_index = jnp.zeros((), jnp.int32)

    def one_row(inputs):
        row_index, lat_offsets, lon_offsets, basis_row, quad_row = inputs
        sources = row_index + HALO + lat_offsets
        begins = HALO + lon_offsets

        def take(source, begin):
            return lax.dynamic_slice(padded, (zero_index, source, begin), (channels, 1, width))[
                :, 0, :
            ]

        support = jax.vmap(take)(sources, begins)
        selector = (basis_row[:, None] == jnp.arange(basis_count, dtype=jnp.int32)[None, :]).astype(
            jnp.float32
        ) * quad_row[:, None]
        aggregate = jnp.einsum(
            "kb,kcj->bcj", selector, support, precision=lax.Precision.HIGHEST
        ).astype(jnp.bfloat16)
        return lax.dot_general(
            disco_weight,
            aggregate,
            (((0, 1), (0, 1)), ((), ())),
            preferred_element_type=jnp.float32,
        )

    row_count = disco_dlat.shape[0]
    stacked = lax.map(
        one_row,
        (jnp.arange(row_count, dtype=jnp.int32), disco_dlat, disco_dlon, disco_basis, disco_quad),
    )
    return jnp.transpose(stacked, (1, 0, 2))


def per_device(
    grid_field,
    disco_dlat,
    disco_dlon,
    disco_basis,
    disco_quad,
    disco_weight,
    norm_gain,
    spectral_filter,
    mix_weight,
):
    lat_count = lax.axis_size("lat")
    lon_count = lax.axis_size("lon")
    channels, lat_local, lon_local = grid_field.shape
    lat_total = lat_local * lat_count
    lon_total = lon_local * lon_count
    mode_count = M_DEV * lat_count
    chan_local = channels // lon_count
    lat_index = lax.axis_index("lat")
    lon_index = lax.axis_index("lon")
    wrapped = padded_2(grid_field, (("lat", 1), ("lon", 2)), HALO)
    global_rows = lat_index * lat_local + jnp.arange(lat_local + 2 * HALO, dtype=jnp.int32) - HALO
    inside = (global_rows >= 0) & (global_rows < lat_total)
    padded = jnp.where(inside[None, :, None], wrapped, 0.0)
    after_conv = grid_field + disco_rows(
        padded, disco_dlat, disco_dlon, disco_basis, disco_quad, disco_weight, lon_local
    )
    mean_square = jnp.mean(after_conv * after_conv, axis=0, keepdims=True)
    normed = after_conv * lax.rsqrt(mean_square + 1e-06) * norm_gain[:, None, None]
    lon_pos = jnp.arange(lon_total, dtype=jnp.int32)
    mode_pos = jnp.arange(mode_count, dtype=jnp.int32)
    phase = (lon_pos[:, None] * mode_pos[None, :] % lon_total).astype(jnp.float32) * (
        2.0 * math.pi / lon_total
    )
    cos_part = jnp.cos(phase)
    sin_part = jnp.sin(phase)
    forward_table = jnp.concatenate([cos_part, -sin_part], axis=1) * (2.0 * math.pi / lon_total)
    mode_weight = jnp.where(mode_pos == 0, 1.0, 2.0).astype(jnp.float32)[None, :]
    inverse_table = jnp.transpose(
        jnp.concatenate([cos_part * mode_weight, -sin_part * mode_weight], axis=1)
    )
    portion = lax.all_to_all(normed, "lon", split_axis=0, concat_axis=2, tiled=True)
    result = jnp.einsum("crj,jq->qcr", portion, forward_table, precision=lax.Precision.HIGHEST)
    fourier = result.reshape(2, mode_count, portion.shape[0], portion.shape[1])
    table = legendre_table(lat_index * M_DEV, M_DEV, mode_count, mode_count, lat_total)
    lat_pos = jnp.arange(lat_total, dtype=jnp.float32)
    quad_weight = math.pi / lat_total * jnp.sin(math.pi * (lat_pos + 0.5) / lat_total)
    local_filter = lax.dynamic_slice_in_dim(spectral_filter, lon_index * chan_local, chan_local, 0)
    weighted = lax.all_to_all(fourier, "lat", split_axis=1, concat_axis=3, tiled=True) * quad_weight
    spectra = jnp.einsum("rmck,lmk->rmcl", weighted, table, precision=lax.Precision.HIGHEST)
    filtered = spectra * local_filter[None, None]
    synthesis = jnp.einsum("rmcl,lmk->rmck", filtered, table, precision=lax.Precision.HIGHEST)
    returned = lax.all_to_all(synthesis, "lat", split_axis=3, concat_axis=1, tiled=True)
    wave_field = jnp.einsum(
        "qcr,qj->crj",
        returned.reshape(2 * mode_count, chan_local, lat_local),
        inverse_table,
        precision=lax.Precision.HIGHEST,
    )
    activated_local = jax.nn.gelu(wave_field, approximate=True).astype(jnp.bfloat16)
    activated = lax.all_to_all(activated_local, "lon", split_axis=2, concat_axis=0, tiled=True)
    mixed = lax.dot_general(
        mix_weight, activated, (((0,), (0,)), ((), ())), preferred_element_type=jnp.float32
    )
    return after_conv + mixed


def solution(mesh):
    placed = (
        P(None, "lat", "lon"),
        P("lat", None),
        P("lat", None),
        P("lat", None),
        P("lat", None),
        P(),
        P(),
        P(),
        P(),
    )
    return jax.shard_map(
        per_device, mesh=mesh, in_specs=placed, out_specs=P(None, "lat", "lon"), check_vma=False
    )
```

profile of v0, /device:TPU:0, one launch (start us, length us, event | category | flops | bytes accessed | tf_op | source)
XLA Modules:
  0.0 368.7 jit_solution(16414946515964665758)
XLA Ops:
  9.4 14.1 %collective-permute-done = f32[384,2,128]{0,1,2:T(2,128)} collective-permute-done((f32[384,2,128]{0,1,2:T(2,128)}, f32[384,2,128]{0,1,2:T(2,128)}, u32[]{:S(2)}, u32[]{:S(2)}) %collective-permute-start) | collective-permute-done | bytes 393248 | tf_op jit(solution)/shard_map/ppermute | solution.py:18
  32.9 146.3 %while.33 = (s32[]{:T(128)}, f32[8,384,128]{1,2,0:T(8,128)}, s32[8,16]{1,0:T(8,128)}, f32[8,16]{1,0:T(8,128)}, s32[8]{0:T(128)S(1)}, /*index=5*/s32[8,16]{1,0:T(...) while((s32[]{:T(128)}, f32[8,384,128]{1,2,0:T(8,128)}, ...), condition=%wide.region_1.2_spmd, body=%wide.region_0.1_spmd.sunk | while | flops 188940624 | bytes 22611376 | solution.py:106
  35.0 6.6 %gather_fusion = f32[16,384,128]{1,0,2:T(8,128)} fusion(f32[384,12,132]{0,1,2:T(8,128)S(1)} %get-tuple-element.853, s32[16]{0:T(128)S(1)} %or_bitcast_fusion.2), kind=kCustom, calls=%fused_computation.clone.1 | custom fusion | bytes 6291648 | tf_op jit(solution)/shard_map/while/body/eval_jaxpr/vmap()/gather | solution.py:87
  41.5 3.6 copy.119
  46.5 3.6 convolution_convert_fusion.2
  53.3 6.6 %gather_fusion = f32[16,384,128]{1,0,2:T(8,128)} fusion(f32[384,12,132]{0,1,2:T(8,128)S(1)} %get-tuple-element.853, s32[16]{0:T(128)S(1)} %or_bitcast_fusion.2), kind=kCustom, calls=%fused_computation.clone.1 | custom fusion | bytes 6291648 | tf_op jit(solution)/shard_map/while/body/eval_jaxpr/vmap()/gather | solution.py:87
  59.8 3.6 copy.119
  64.8 3.6 convolution_convert_fusion.2
  71.6 6.6 %gather_fusion = f32[16,384,128]{1,0,2:T(8,128)} fusion(f32[384,12,132]{0,1,2:T(8,128)S(1)} %get-tuple-element.853, s32[16]{0:T(128)S(1)} %or_bitcast_fusion.2), kind=kCustom, calls=%fused_computation.clone.1 | custom fusion | bytes 6291648 | tf_op jit(solution)/shard_map/while/body/eval_jaxpr/vmap()/gather | solution.py:87
  78.1 3.6 copy.119
  83.1 3.6 convolution_convert_fusion.2
  89.8 6.6 %gather_fusion = f32[16,384,128]{1,0,2:T(8,128)} fusion(f32[384,12,132]{0,1,2:T(8,128)S(1)} %get-tuple-element.853, s32[16]{0:T(128)S(1)} %or_bitcast_fusion.2), kind=kCustom, calls=%fused_computation.clone.1 | custom fusion | bytes 6291648 | tf_op jit(solution)/shard_map/while/body/eval_jaxpr/vmap()/gather | solution.py:87
  96.4 3.6 copy.119
  101.4 3.6 convolution_convert_fusion.2
  108.1 6.6 %gather_fusion = f32[16,384,128]{1,0,2:T(8,128)} fusion(f32[384,12,132]{0,1,2:T(8,128)S(1)} %get-tuple-element.853, s32[16]{0:T(128)S(1)} %or_bitcast_fusion.2), kind=kCustom, calls=%fused_computation.clone.1 | custom fusion | bytes 6291648 | tf_op jit(solution)/shard_map/while/body/eval_jaxpr/vmap()/gather | solution.py:87
  114.7 3.6 copy.119
  119.7 3.6 convolution_convert_fusion.2
  126.4 6.6 %gather_fusion = f32[16,384,128]{1,0,2:T(8,128)} fusion(f32[384,12,132]{0,1,2:T(8,128)S(1)} %get-tuple-element.853, s32[16]{0:T(128)S(1)} %or_bitcast_fusion.2), kind=kCustom, calls=%fused_computation.clone.1 | custom fusion | bytes 6291648 | tf_op jit(solution)/shard_map/while/body/eval_jaxpr/vmap()/gather | solution.py:87
  132.9 3.6 copy.119
  144.7 6.6 %gather_fusion = f32[16,384,128]{1,0,2:T(8,128)} fusion(f32[384,12,132]{0,1,2:T(8,128)S(1)} %get-tuple-element.853, s32[16]{0:T(128)S(1)} %or_bitcast_fusion.2), kind=kCustom, calls=%fused_computation.clone.1 | custom fusion | bytes 6291648 | tf_op jit(solution)/shard_map/while/body/eval_jaxpr/vmap()/gather | solution.py:87
  151.2 3.6 copy.119
  156.2 3.6 convolution_convert_fusion.2
  162.9 6.6 %gather_fusion = f32[16,384,128]{1,0,2:T(8,128)} fusion(f32[384,12,132]{0,1,2:T(8,128)S(1)} %get-tuple-element.853, s32[16]{0:T(128)S(1)} %or_bitcast_fusion.2), kind=kCustom, calls=%fused_computation.clone.1 | custom fusion | bytes 6291648 | tf_op jit(solution)/shard_map/while/body/eval_jaxpr/vmap()/gather | solution.py:87
  169.5 3.6 copy.119
  174.5 3.6 convolution_convert_fusion.2
  184.9 3.7 %all-to-all-start = ((f32[384,8,128]{2,1,0:T(8,128)}), f32[384,8,128]{2,1,0:T(8,128)S(1)}, u32[]{:S(2)}, u32[]{:S(2)}) async-start(f32[384,8,128]{2,1,0:T(8,128)} %copy.83), calls=%async_computation | async-start | bytes 3145728 | tf_op jit(solution)/shard_map/all_to_all | solution.py:154
  192.8 15.7 %all-to-all-done = f32[384,8,128]{2,1,0:T(8,128)S(1)} async-done(((f32[384,8,128]{2,1,0:T(8,128)}), f32[384,8,128]{2,1,0:T(8,128)S(1)}, u32[]{:S(2)}, u32[]{:S(2)}) %all-to-all-start) | async-done | bytes 1572896 | tf_op jit(solution)/shard_map/all_to_all | solution.py:154
  216.6 4.6 %all-to-all-start.1 = ((f32[2,64,96,8]{2,3,0,1:T(8,128)}), f32[2,64,96,8]{2,3,0,1:T(8,128)S(1)}, u32[]{:S(2)}, u32[]{:S(2)}) async-start(f32[2,64,96,8]{2,3,0,1:T(8,128)} %copy.85), calls=%async_computation.1 | async-start | bytes 1048576 | tf_op jit(solution)/shard_map/all_to_all | solution.py:161
  221.3 95.3 %while.34 = (s32[]{:T(128)}, f32[8,64]{1,0:T(8,128)S(1)}, f32[8,64]{1,0:T(8,128)S(1)}, f32[8,8,8,64]{3,2,1,0:T(8,128)S(1)}, s32[8,8]{1,0:T(8,128)S(1)}, /*index=...) while((s32[]{:T(128)}, f32[8,64]{1,0:T(8,128)S(1)}, ...), condition=%wide.region_4.5_spmd.clone.clone.clone.clone, body=%wide.region_3.4_spmd.clone.clone.clone.clone.sunk | while | flops 93138 | bytes 238507 | solution.py:70
  320.2 6.0 %all-to-all-start.2 = ((f32[2,8,96,64]{2,0,1,3:T(2,128)}), f32[2,8,96,64]{2,0,1,3:T(2,128)S(1)}, u32[]{:S(2)}, u32[]{:S(2)}) async-start(f32[2,8,96,64]{2,0,1,3:T(2,128)} %copy.91), calls=%async_computation.2 | async-start | bytes 1048576 | tf_op jit(solution)/shard_map/all_to_all | solution.py:165
  327.3 12.6 %all-to-all-done.2 = f32[2,8,96,64]{2,0,1,3:T(2,128)S(1)} async-done(((f32[2,8,96,64]{2,0,1,3:T(2,128)}), f32[2,8,96,64]{2,0,1,3:T(2,128)S(1)}, u32[]{:S(2)}, u32[]{:S(2)}) %all-to-all-start.2) | async-done | bytes 393248 | tf_op jit(solution)/shard_map/all_to_all | solution.py:165
  345.2 17.6 %all_to_all.69 = bf16[96,8,512]{0,1,2:T(8,128)(2,1)} all-to-all(bf16[96,8,512]{0,1,2:T(8,128)(2,1)S(1)} %copy.94), channel_id=1, replica_groups=mesh['lat'=8,'lon'=4] {'lon'}, dimensions={2} | all-to-all | bytes 1572864 | tf_op jit(solution)/shard_map/all_to_all | solution.py:173
  (349 shorter events, 140.2 us)
Async XLA Ops:
  0.0 365.0 %copy-start = (bf16[384,384]{1,0:T(8,128)(2,1)S(1)}, bf16[384,384]{1,0:T(8,128)(2,1)}, u32[]{:S(2)}) copy-start(bf16[384,384]{1,0:T(8,128)(2,1)} %param.21) | copy-start | bytes 884740
  2.0 24.4 %copy-start.3 = (f32[384,8,128]{0,1,2:T(8,128)}, f32[384,8,128]{0,1,2:T(8,128)S(1)}, u32[]{:S(2)}) copy-start(f32[384,8,128]{0,1,2:T(8,128)S(1)} %copy.78) | copy-start | bytes 4718596
  3.3 24.9 %copy-start.4 = (f32[384,8,128]{2,1,0:T(8,128)S(1)}, f32[384,8,128]{2,1,0:T(8,128)}, u32[]{:S(2)}) copy-start(f32[384,8,128]{2,1,0:T(8,128)} %param.13) | copy-start | bytes 4718596
  3.3 20.1 %collective-permute-start = (f32[384,2,128]{0,1,2:T(2,128)}, f32[384,2,128]{0,1,2:T(2,128)}, u32[]{:S(2)}, u32[]{:S(2)}) collective-permute-start(f32[384,2,128]{0,1,2:T(2,128)} %get-tuple-element.570), channel_id=1, source_target_pairs={{0,4},{4,8},{8,12},{12,16},{16,20},{20,24},{24,28},{28,0},{1,5},{5... | collective-permute-start | bytes 1179656 | tf_op jit(solution)/shard_map/ppermute | solution.py:18
  6.3 19.3 %collective-permute-start.1 = (f32[384,2,128]{0,1,2:T(2,128)}, f32[384,2,128]{0,1,2:T(2,128)}, u32[]{:S(2)}, u32[]{:S(2)}) collective-permute-start(f32[384,2,128]{0,1,2:T(2,128)} %get-tuple-element.571), channel_id=1, source_target_pairs={{4,0},{8,4},{12,8},{16,12},{20,16},{24,20},{28,24},{0,28},{5,1},{9... | collective-permute-start | bytes 1179656 | tf_op jit(solution)/shard_map/ppermute | solution.py:20
  26.4 3.6 collective-permute-start.2
  26.5 4.1 %collective-permute-start.3 = (f32[384,12,2]{0,1,2:T(8,128)S(1)}, f32[384,12,2]{0,1,2:T(8,128)}, u32[]{:S(2)}, u32[]{:S(2)}) collective-permute-start(f32[384,12,2]{0,1,2:T(8,128)S(1)} %get-tuple-element.569), channel_id=1, source_target_pairs={{1,0},{2,1},{3,2},{0,3},{5,4},{6,5},{7,6},{4,7},{9,8},{10,9},{11,1... | collective-permute-start | bytes 110600 | tf_op jit(solution)/shard_map/ppermute | solution.py:20
  30.0 0.6 copy-start.6
  46.5 3.6 copy-start.1
  64.8 3.6 copy-start.1
  83.1 3.6 copy-start.1
  101.4 3.6 copy-start.1
  119.7 3.6 copy-start.1
  137.9 3.6 copy-start.1
  156.2 3.6 copy-start.1
  174.5 3.6 copy-start.1
  179.2 2.4 copy-start.2
  179.2 2.4 copy-start.7
  184.9 23.6 %all-to-all-start = ((f32[384,8,128]{2,1,0:T(8,128)}), f32[384,8,128]{2,1,0:T(8,128)S(1)}, u32[]{:S(2)}, u32[]{:S(2)}) async-start(f32[384,8,128]{2,1,0:T(8,128)} %copy.83), calls=%async_computation | async-start | bytes 3145728 | tf_op jit(solution)/shard_map/all_to_all | solution.py:154
  215.5 5.7 %copy-start.5 = (f32[8,8,8,64]{3,2,1,0:T(8,128)S(1)}, f32[8,8,8,64]{3,2,1,0:T(8,128)}, u32[]{:S(2)}) copy-start(f32[8,8,8,64]{3,2,1,0:T(8,128)} %custom-call.6) | copy-start | bytes 393220
  216.6 101.1 %all-to-all-start.1 = ((f32[2,64,96,8]{2,3,0,1:T(8,128)}), f32[2,64,96,8]{2,3,0,1:T(8,128)S(1)}, u32[]{:S(2)}, u32[]{:S(2)}) async-start(f32[2,64,96,8]{2,3,0,1:T(8,128)} %copy.85), calls=%async_computation.1 | async-start | bytes 1048576 | tf_op jit(solution)/shard_map/all_to_all | solution.py:161
  320.2 19.7 %all-to-all-start.2 = ((f32[2,8,96,64]{2,0,1,3:T(2,128)}), f32[2,8,96,64]{2,0,1,3:T(2,128)S(1)}, u32[]{:S(2)}, u32[]{:S(2)}) async-start(f32[2,8,96,64]{2,0,1,3:T(2,128)} %copy.91), calls=%async_computation.2 | async-start | bytes 1048576 | tf_op jit(solution)/shard_map/all_to_all | solution.py:165
where the time goes:
time: 371 us; the launch traced here: 369 us
  local copies, waits for them, and re-layouts  126 us (34%)
  other arithmetic  63.9 us (17%)
  loops' own time  47.8 us (13%)
  matrix products  46.6 us (13%)
  waiting for transfers between devices  44.6 us (12%)
  starting transfers between devices  22.2 us (6%)
  blocking collectives  17.6 us (5%)
    gather x16, local copies, waits for them, and re-layouts, take(): lax.dynamic_slice(padded, (zero_index, source, begin), (channels, 1, width))  81.2 us
    another operation x1, loops' own time, legendre_table(): lax.scan(advance, (empty, empty), jnp.arange(degrees, dtype=jnp.int32), u...  42.2 us
    gt x64, other arithmetic, advance(): degree > orders[:, None]  40.5 us
    dot_general x8, matrix products, one_row(): jnp.einsum('kb,kcj->bcj', selector, support, precision=lax.Precision.HIGH...  28.7 us
    all_to_all x1, blocking collectives, per_device(): lax.all_to_all(activated_local, 'lon', split_axis=2, concat_axis=0, tiled...  17.6 us
    all_to_all x1, waiting for transfers between devices, per_device(): lax.all_to_all(normed, 'lon', split_axis=0, concat_axis=2, tiled=True)  15.7 us
    ppermute x2, waiting for transfers between devices, padded_2(): lax.ppermute(tail, axis, [(i, (i + 1) % count) for i in range(count)])  14.1 us
    all_to_all x1, waiting for transfers between devices, per_device(): lax.all_to_all(synthesis, 'lat', split_axis=3, concat_axis=1, tiled=True)  12.6 us
  transfers between devices with their start and end apart: 7, of which 5 were waited for; matrix products, arithmetic and copies ran while one was open for 17% of the time, Pallas kernels for 0%

commit v1 on v0

--- a/solution.py
+++ b/solution.py
@@ -6,6 +6,20 @@
 
 M_DEV = 8
 HALO = 2
+
+
+def review_the_positions(original, out_dim, matrix):
+    r_now = original.shape
+    taken_in = original.reshape(
+        *r_now[:out_dim], matrix, r_now[out_dim] // matrix, *r_now[out_dim + 1 :]
+    )
+    return jnp.moveaxis(taken_in, out_dim, 0)
+
+
+def raise_layers_all(local, d_out):
+    part_now = list(local.shape[1:])
+    part_now[d_out] *= local.shape[0]
+    return jnp.moveaxis(local, 0, d_out).reshape(part_now)
 
 
 def padded_2(cells, sides, width):
@@ -170,7 +184,20 @@
         precision=lax.Precision.HIGHEST,
     )
     activated_local = jax.nn.gelu(wave_field, approximate=True).astype(jnp.bfloat16)
-    activated = lax.all_to_all(activated_local, "lon", split_axis=2, concat_axis=0, tiled=True)
+
+    def save_vectors(array_in, dev_axis, t0, m):
+        z, long_array = (lax.psum(1, dev_axis), lax.axis_index(dev_axis))
+        step_out = review_the_positions(array_in, t0, z)
+        row_list = [step_out[long_array]]
+        for jj in range(1, z):
+            base_arr = step_out[(long_array + jj) % z]
+            row_list.append(
+                lax.ppermute(base_arr, dev_axis, [(ix, (ix + jj) % z) for ix in range(z)])
+            )
+        step_out = jnp.stack(row_list, axis=0)[(long_array - jnp.arange(z)) % z]
+        return raise_layers_all(step_out, m)
+
+    activated = save_vectors(activated_local, "lon", 2, 0)
     mixed = lax.dot_general(
         mix_weight, activated, (((0,), (0,)), ((), ())), preferred_element_type=jnp.float32
     )

time: 371 us -> 360 us (0.970)
  blocking collectives: 17.6 us -> 0 us
  waiting for transfers between devices: 44.6 us -> 52 us
    all_to_all x1 -> x0, blocking collectives: 17.6 us -> none  [per_device(): lax.all_to_all(activated_local, 'lon', split_axis=2, concat_axis=0, tiled...]
    ppermute x0 -> x3, waiting for transfers between devices: none -> 7.44 us  [save_vectors(): lax.ppermute(base_arr, dev_axis, [(ix, (ix + jj) % z) for ix in range(z)])]
  transfers between devices with their start and end apart: 7 -> 10, of which waited for: 5 -> 8; matrix products, arithmetic and copies ran while one was open for 17% -> 17% of each run, Pallas kernels for 0% -> 0%
where the time goes in v1:
time: 360 us; the launch traced here: 356 us
  local copies, waits for them, and re-layouts  123 us (34%)
  other arithmetic  63.4 us (18%)
  waiting for transfers between devices  52 us (14%)
  loops' own time  46.8 us (13%)
  matrix products  46 us (13%)
  starting transfers between devices  24.6 us (7%)
    gather x16, local copies, waits for them, and re-layouts, take(): lax.dynamic_slice(padded, (zero_index, source, begin), (channels, 1, width))  81.1 us
    another operation x1, loops' own time, legendre_table(): lax.scan(advance, (empty, empty), jnp.arange(degrees, dtype=jnp.int32), u...  41.6 us
    gt x64, other arithmetic, advance(): degree > orders[:, None]  39.9 us
    dot_general x8, matrix products, one_row(): jnp.einsum('kb,kcj->bcj', selector, support, precision=lax.Precision.HIGH...  28.7 us
    all_to_all x1, waiting for transfers between devices, per_device(): lax.all_to_all(normed, 'lon', split_axis=0, concat_axis=2, tiled=True)  15.7 us
    ppermute x2, waiting for transfers between devices, padded_2(): lax.ppermute(tail, axis, [(i, (i + 1) % count) for i in range(count)])  14.1 us
    all_to_all x1, waiting for transfers between devices, per_device(): lax.all_to_all(synthesis, 'lat', split_axis=3, concat_axis=1, tiled=True)  12.6 us
    dot_general x8, matrix products, one_row(): lax.dot_general(disco_weight, aggregate, (((0, 1), (0, 1)), ((), ())), pr...  8.78 us
  transfers between devices with their start and end apart: 10, of which 8 were waited for; matrix products, arithmetic and copies ran while one was open for 17% of the time, Pallas kernels for 0%

profile of v1, /device:TPU:0, one launch (start us, length us, event | category | flops | bytes accessed | tf_op | source)
XLA Modules:
  0.0 356.3 jit_solution(11122057626709813915)
XLA Ops:
  9.4 14.1 %collective-permute-done = f32[384,2,128]{0,1,2:T(2,128)} collective-permute-done((f32[384,2,128]{0,1,2:T(2,128)}, f32[384,2,128]{0,1,2:T(2,128)}, u32[]{:S(2)}, u32[]{:S(2)}) %collective-permute-start) | collective-permute-done | bytes 393248 | tf_op jit(solution)/shard_map/ppermute | solution.py:32
  32.9 145.7 %while.33 = (s32[]{:T(128)}, f32[8,384,128]{1,2,0:T(8,128)}, s32[8,16]{1,0:T(8,128)}, f32[8,16]{1,0:T(8,128)}, s32[8]{0:T(128)S(1)}, /*index=5*/s32[8,16]{1,0:T(...) while((s32[]{:T(128)}, f32[8,384,128]{1,2,0:T(8,128)}, ...), condition=%wide.region_1.2_spmd, body=%wide.region_0.1_spmd.sunk | while | flops 188940624 | bytes 22611376 | solution.py:120
  34.9 6.5 %gather_fusion = f32[16,384,128]{1,0,2:T(8,128)} fusion(f32[384,12,132]{0,1,2:T(8,128)S(1)} %get-tuple-element.857, s32[16]{0:T(128)S(1)} %or_bitcast_fusion.2), kind=kCustom, calls=%fused_computation.clone.1 | custom fusion | bytes 6291648 | tf_op jit(solution)/shard_map/while/body/eval_jaxpr/vmap()/gather | solution.py:101
  41.5 3.6 %copy.90 = f32[16,384,128]{2,0,1:T(8,128)} copy(f32[16,384,128]{1,0,2:T(8,128)} %gather_fusion) | data formatting | bytes 6291456 | tf_op jit(solution)/shard_map/while/body/eval_jaxpr/vmap()/gather | solution.py:101
  46.5 3.6 %convolution_convert_fusion.2 = bf16[4,384,128]{2,0,1:T(4,128)(2,1)S(1)} fusion(f32[16,384,128]{2,0,1:T(8,128)} %copy.90, f32[16]{0:T(128)S(1)} %fusion.121, s32[16]{0:T(128)S(1)} %fusion.122), kind=kOutput, calls=%fused_computation.7.clone.1 | convolution fusion | flops 37945472 | bytes 3539072 | tf_op jit(solution)/shard_map/while/body/eval_jaxpr/kb,kcj->bcj/dot_general | solution.py:109
  53.2 6.5 %gather_fusion = f32[16,384,128]{1,0,2:T(8,128)} fusion(f32[384,12,132]{0,1,2:T(8,128)S(1)} %get-tuple-element.857, s32[16]{0:T(128)S(1)} %or_bitcast_fusion.2), kind=kCustom, calls=%fused_computation.clone.1 | custom fusion | bytes 6291648 | tf_op jit(solution)/shard_map/while/body/eval_jaxpr/vmap()/gather | solution.py:101
  59.7 3.6 %copy.90 = f32[16,384,128]{2,0,1:T(8,128)} copy(f32[16,384,128]{1,0,2:T(8,128)} %gather_fusion) | data formatting | bytes 6291456 | tf_op jit(solution)/shard_map/while/body/eval_jaxpr/vmap()/gather | solution.py:101
  64.7 3.6 %convolution_convert_fusion.2 = bf16[4,384,128]{2,0,1:T(4,128)(2,1)S(1)} fusion(f32[16,384,128]{2,0,1:T(8,128)} %copy.90, f32[16]{0:T(128)S(1)} %fusion.121, s32[16]{0:T(128)S(1)} %fusion.122), kind=kOutput, calls=%fused_computation.7.clone.1 | convolution fusion | flops 37945472 | bytes 3539072 | tf_op jit(solution)/shard_map/while/body/eval_jaxpr/kb,kcj->bcj/dot_general | solution.py:109
  71.4 6.5 %gather_fusion = f32[16,384,128]{1,0,2:T(8,128)} fusion(f32[384,12,132]{0,1,2:T(8,128)S(1)} %get-tuple-element.857, s32[16]{0:T(128)S(1)} %or_bitcast_fusion.2), kind=kCustom, calls=%fused_computation.clone.1 | custom fusion | bytes 6291648 | tf_op jit(solution)/shard_map/while/body/eval_jaxpr/vmap()/gather | solution.py:101
  77.9 3.6 %copy.90 = f32[16,384,128]{2,0,1:T(8,128)} copy(f32[16,384,128]{1,0,2:T(8,128)} %gather_fusion) | data formatting | bytes 6291456 | tf_op jit(solution)/shard_map/while/body/eval_jaxpr/vmap()/gather | solution.py:101
  82.9 3.6 %convolution_convert_fusion.2 = bf16[4,384,128]{2,0,1:T(4,128)(2,1)S(1)} fusion(f32[16,384,128]{2,0,1:T(8,128)} %copy.90, f32[16]{0:T(128)S(1)} %fusion.121, s32[16]{0:T(128)S(1)} %fusion.122), kind=kOutput, calls=%fused_computation.7.clone.1 | convolution fusion | flops 37945472 | bytes 3539072 | tf_op jit(solution)/shard_map/while/body/eval_jaxpr/kb,kcj->bcj/dot_general | solution.py:109
  89.6 6.5 %gather_fusion = f32[16,384,128]{1,0,2:T(8,128)} fusion(f32[384,12,132]{0,1,2:T(8,128)S(1)} %get-tuple-element.857, s32[16]{0:T(128)S(1)} %or_bitcast_fusion.2), kind=kCustom, calls=%fused_computation.clone.1 | custom fusion | bytes 6291648 | tf_op jit(solution)/shard_map/while/body/eval_jaxpr/vmap()/gather | solution.py:101
  96.1 3.6 %copy.90 = f32[16,384,128]{2,0,1:T(8,128)} copy(f32[16,384,128]{1,0,2:T(8,128)} %gather_fusion) | data formatting | bytes 6291456 | tf_op jit(solution)/shard_map/while/body/eval_jaxpr/vmap()/gather | solution.py:101
  101.1 3.6 %convolution_convert_fusion.2 = bf16[4,384,128]{2,0,1:T(4,128)(2,1)S(1)} fusion(f32[16,384,128]{2,0,1:T(8,128)} %copy.90, f32[16]{0:T(128)S(1)} %fusion.121, s32[16]{0:T(128)S(1)} %fusion.122), kind=kOutput, calls=%fused_computation.7.clone.1 | convolution fusion | flops 37945472 | bytes 3539072 | tf_op jit(solution)/shard_map/while/body/eval_jaxpr/kb,kcj->bcj/dot_general | solution.py:109
  107.8 6.5 %gather_fusion = f32[16,384,128]{1,0,2:T(8,128)} fusion(f32[384,12,132]{0,1,2:T(8,128)S(1)} %get-tuple-element.857, s32[16]{0:T(128)S(1)} %or_bitcast_fusion.2), kind=kCustom, calls=%fused_computation.clone.1 | custom fusion | bytes 6291648 | tf_op jit(solution)/shard_map/while/body/eval_jaxpr/vmap()/gather | solution.py:101
  114.3 3.6 %copy.90 = f32[16,384,128]{2,0,1:T(8,128)} copy(f32[16,384,128]{1,0,2:T(8,128)} %gather_fusion) | data formatting | bytes 6291456 | tf_op jit(solution)/shard_map/while/body/eval_jaxpr/vmap()/gather | solution.py:101
  119.3 3.6 %convolution_convert_fusion.2 = bf16[4,384,128]{2,0,1:T(4,128)(2,1)S(1)} fusion(f32[16,384,128]{2,0,1:T(8,128)} %copy.90, f32[16]{0:T(128)S(1)} %fusion.121, s32[16]{0:T(128)S(1)} %fusion.122), kind=kOutput, calls=%fused_computation.7.clone.1 | convolution fusion | flops 37945472 | bytes 3539072 | tf_op jit(solution)/shard_map/while/body/eval_jaxpr/kb,kcj->bcj/dot_general | solution.py:109
  126.0 6.5 %gather_fusion = f32[16,384,128]{1,0,2:T(8,128)} fusion(f32[384,12,132]{0,1,2:T(8,128)S(1)} %get-tuple-element.857, s32[16]{0:T(128)S(1)} %or_bitcast_fusion.2), kind=kCustom, calls=%fused_computation.clone.1 | custom fusion | bytes 6291648 | tf_op jit(solution)/shard_map/while/body/eval_jaxpr/vmap()/gather | solution.py:101
  132.5 3.6 %copy.90 = f32[16,384,128]{2,0,1:T(8,128)} copy(f32[16,384,128]{1,0,2:T(8,128)} %gather_fusion) | data formatting | bytes 6291456 | tf_op jit(solution)/shard_map/while/body/eval_jaxpr/vmap()/gather | solution.py:101
  137.5 3.6 %convolution_convert_fusion.2 = bf16[4,384,128]{2,0,1:T(4,128)(2,1)S(1)} fusion(f32[16,384,128]{2,0,1:T(8,128)} %copy.90, f32[16]{0:T(128)S(1)} %fusion.121, s32[16]{0:T(128)S(1)} %fusion.122), kind=kOutput, calls=%fused_computation.7.clone.1 | convolution fusion | flops 37945472 | bytes 3539072 | tf_op jit(solution)/shard_map/while/body/eval_jaxpr/kb,kcj->bcj/dot_general | solution.py:109
  144.2 6.5 %gather_fusion = f32[16,384,128]{1,0,2:T(8,128)} fusion(f32[384,12,132]{0,1,2:T(8,128)S(1)} %get-tuple-element.857, s32[16]{0:T(128)S(1)} %or_bitcast_fusion.2), kind=kCustom, calls=%fused_computation.clone.1 | custom fusion | bytes 6291648 | tf_op jit(solution)/shard_map/while/body/eval_jaxpr/vmap()/gather | solution.py:101
  150.7 3.6 %copy.90 = f32[16,384,128]{2,0,1:T(8,128)} copy(f32[16,384,128]{1,0,2:T(8,128)} %gather_fusion) | data formatting | bytes 6291456 | tf_op jit(solution)/shard_map/while/body/eval_jaxpr/vmap()/gather | solution.py:101
  155.7 3.6 %convolution_convert_fusion.2 = bf16[4,384,128]{2,0,1:T(4,128)(2,1)S(1)} fusion(f32[16,384,128]{2,0,1:T(8,128)} %copy.90, f32[16]{0:T(128)S(1)} %fusion.121, s32[16]{0:T(128)S(1)} %fusion.122), kind=kOutput, calls=%fused_computation.7.clone.1 | convolution fusion | flops 37945472 | bytes 3539072 | tf_op jit(solution)/shard_map/while/body/eval_jaxpr/kb,kcj->bcj/dot_general | solution.py:109
  162.4 6.5 %gather_fusion = f32[16,384,128]{1,0,2:T(8,128)} fusion(f32[384,12,132]{0,1,2:T(8,128)S(1)} %get-tuple-element.857, s32[16]{0:T(128)S(1)} %or_bitcast_fusion.2), kind=kCustom, calls=%fused_computation.clone.1 | custom fusion | bytes 6291648 | tf_op jit(solution)/shard_map/while/body/eval_jaxpr/vmap()/gather | solution.py:101
  169.0 3.6 %copy.90 = f32[16,384,128]{2,0,1:T(8,128)} copy(f32[16,384,128]{1,0,2:T(8,128)} %gather_fusion) | data formatting | bytes 6291456 | tf_op jit(solution)/shard_map/while/body/eval_jaxpr/vmap()/gather | solution.py:101
  184.3 3.7 %all-to-all-start = ((f32[384,8,128]{2,1,0:T(8,128)}), f32[384,8,128]{2,1,0:T(8,128)S(1)}, u32[]{:S(2)}, u32[]{:S(2)}) async-start(f32[384,8,128]{2,1,0:T(8,128)} %copy.57), calls=%async_computation | async-start | bytes 3145728 | tf_op jit(solution)/shard_map/all_to_all | solution.py:168
  192.2 15.7 %all-to-all-done = f32[384,8,128]{2,1,0:T(8,128)S(1)} async-done(((f32[384,8,128]{2,1,0:T(8,128)}), f32[384,8,128]{2,1,0:T(8,128)S(1)}, u32[]{:S(2)}, u32[]{:S(2)}) %all-to-all-start) | async-done | bytes 1572896 | tf_op jit(solution)/shard_map/all_to_all | solution.py:168
  216.1 4.6 %all-to-all-start.1 = ((f32[2,64,96,8]{2,3,0,1:T(8,128)}), f32[2,64,96,8]{2,3,0,1:T(8,128)S(1)}, u32[]{:S(2)}, u32[]{:S(2)}) async-start(f32[2,64,96,8]{2,3,0,1:T(8,128)} %copy.59), calls=%async_computation.1 | async-start | bytes 1048576 | tf_op jit(solution)/shard_map/all_to_all | solution.py:175
  220.7 94.3 %while.34 = (s32[]{:T(128)}, f32[8,64]{1,0:T(8,128)S(1)}, f32[8,64]{1,0:T(8,128)S(1)}, f32[8,8,8,64]{3,2,1,0:T(8,128)S(1)}, s32[8,8]{1,0:T(8,128)S(1)}, /*index=...) while((s32[]{:T(128)}, f32[8,64]{1,0:T(8,128)S(1)}, ...), condition=%wide.region_4.5_spmd.clone.clone.clone.clone, body=%wide.region_3.4_spmd.clone.clone.clone.clone.sunk | while | flops 93138 | bytes 238507 | solution.py:84
  318.6 6.0 %all-to-all-start.2 = ((f32[2,8,96,64]{2,0,1,3:T(2,128)}), f32[2,8,96,64]{2,0,1,3:T(2,128)S(1)}, u32[]{:S(2)}, u32[]{:S(2)}) async-start(f32[2,8,96,64]{2,0,1,3:T(2,128)} %copy.65), calls=%async_computation.2 | async-start | bytes 1048576 | tf_op jit(solution)/shard_map/all_to_all | solution.py:179
  325.7 12.6 %all-to-all-done.2 = f32[2,8,96,64]{2,0,1,3:T(2,128)S(1)} async-done(((f32[2,8,96,64]{2,0,1,3:T(2,128)}), f32[2,8,96,64]{2,0,1,3:T(2,128)S(1)}, u32[]{:S(2)}, u32[]{:S(2)}) %all-to-all-start.2) | async-done | bytes 393248 | tf_op jit(solution)/shard_map/all_to_all | solution.py:179
  343.3 4.1 %collective-permute-done.4 = bf16[96,8,128]{2,1,0:T(8,128)(2,1)S(1)} collective-permute-done((bf16[96,8,128]{2,1,0:T(8,128)(2,1)S(1)}, bf16[96,8,128]{2,1,0:T(8,128)(2,1)S(1)}, u32[]{:S(2)}, u32[]{:S(2)}) %collective-permute-start.4) | collective-permute-done | bytes 196640 | tf_op jit(solution)/shard_map/ppermute | solution.py:195
  (356 shorter events, 142.3 us)
Async XLA Ops:
  0.0 352.4 %copy-start = (bf16[384,384]{1,0:T(8,128)(2,1)S(1)}, bf16[384,384]{1,0:T(8,128)(2,1)}, u32[]{:S(2)}) copy-start(bf16[384,384]{1,0:T(8,128)(2,1)} %param.21) | copy-start | bytes 884740
  2.0 24.4 %copy-start.3 = (f32[384,8,128]{0,1,2:T(8,128)}, f32[384,8,128]{0,1,2:T(8,128)S(1)}, u32[]{:S(2)}) copy-start(f32[384,8,128]{0,1,2:T(8,128)S(1)} %copy.52) | copy-start | bytes 4718596
  3.4 24.9 %copy-start.4 = (f32[384,8,128]{2,1,0:T(8,128)S(1)}, f32[384,8,128]{2,1,0:T(8,128)}, u32[]{:S(2)}) copy-start(f32[384,8,128]{2,1,0:T(8,128)} %param.13) | copy-start | bytes 4718596
  3.4 20.1 %collective-permute-start = (f32[384,2,128]{0,1,2:T(2,128)}, f32[384,2,128]{0,1,2:T(2,128)}, u32[]{:S(2)}, u32[]{:S(2)}) collective-permute-start(f32[384,2,128]{0,1,2:T(2,128)} %get-tuple-element.570), channel_id=1, source_target_pairs={{0,4},{4,8},{8,12},{12,16},{16,20},{20,24},{24,28},{28,0},{1,5},{5... | collective-permute-start | bytes 1179656 | tf_op jit(solution)/shard_map/ppermute | solution.py:32
  6.4 19.3 %collective-permute-start.1 = (f32[384,2,128]{0,1,2:T(2,128)}, f32[384,2,128]{0,1,2:T(2,128)}, u32[]{:S(2)}, u32[]{:S(2)}) collective-permute-start(f32[384,2,128]{0,1,2:T(2,128)} %get-tuple-element.571), channel_id=1, source_target_pairs={{4,0},{8,4},{12,8},{16,12},{20,16},{24,20},{28,24},{0,28},{5,1},{9... | collective-permute-start | bytes 1179656 | tf_op jit(solution)/shard_map/ppermute | solution.py:34
  26.5 3.6 %collective-permute-start.2 = (f32[384,12,2]{0,1,2:T(8,128)S(1)}, f32[384,12,2]{0,1,2:T(8,128)S(1)}, u32[]{:S(2)}, u32[]{:S(2)}) collective-permute-start(f32[384,12,2]{0,1,2:T(8,128)S(1)} %get-tuple-element.568), channel_id=1, source_target_pairs={{0,1},{1,2},{2,3},{3,0},{4,5},{5,6},{6,7},{7,4},{8,9},{9,10},{10,1... | collective-permute-start | bytes 110600 | tf_op jit(solution)/shard_map/ppermute | solution.py:32
  26.5 4.1 %collective-permute-start.3 = (f32[384,12,2]{0,1,2:T(8,128)S(1)}, f32[384,12,2]{0,1,2:T(8,128)}, u32[]{:S(2)}, u32[]{:S(2)}) collective-permute-start(f32[384,12,2]{0,1,2:T(8,128)S(1)} %get-tuple-element.569), channel_id=1, source_target_pairs={{1,0},{2,1},{3,2},{0,3},{5,4},{6,5},{7,6},{4,7},{9,8},{10,9},{11,1... | collective-permute-start | bytes 110600 | tf_op jit(solution)/shard_map/ppermute | solution.py:34
  30.0 0.6 copy-start.6
  46.5 3.6 %copy-start.1 = (bf16[4,384,384]{2,1,0:T(8,128)(2,1)S(1)}, bf16[4,384,384]{2,1,0:T(8,128)(2,1)}, u32[]{:S(2)}) copy-start(bf16[4,384,384]{2,1,0:T(8,128)(2,1)} %get-tuple-element.858) | copy-start | bytes 3538948 | tf_op jit(solution)/shard_map/while
  64.7 3.6 %copy-start.1 = (bf16[4,384,384]{2,1,0:T(8,128)(2,1)S(1)}, bf16[4,384,384]{2,1,0:T(8,128)(2,1)}, u32[]{:S(2)}) copy-start(bf16[4,384,384]{2,1,0:T(8,128)(2,1)} %get-tuple-element.858) | copy-start | bytes 3538948 | tf_op jit(solution)/shard_map/while
  82.9 3.6 %copy-start.1 = (bf16[4,384,384]{2,1,0:T(8,128)(2,1)S(1)}, bf16[4,384,384]{2,1,0:T(8,128)(2,1)}, u32[]{:S(2)}) copy-start(bf16[4,384,384]{2,1,0:T(8,128)(2,1)} %get-tuple-element.858) | copy-start | bytes 3538948 | tf_op jit(solution)/shard_map/while
  101.1 3.6 %copy-start.1 = (bf16[4,384,384]{2,1,0:T(8,128)(2,1)S(1)}, bf16[4,384,384]{2,1,0:T(8,128)(2,1)}, u32[]{:S(2)}) copy-start(bf16[4,384,384]{2,1,0:T(8,128)(2,1)} %get-tuple-element.858) | copy-start | bytes 3538948 | tf_op jit(solution)/shard_map/while
  119.3 3.6 %copy-start.1 = (bf16[4,384,384]{2,1,0:T(8,128)(2,1)S(1)}, bf16[4,384,384]{2,1,0:T(8,128)(2,1)}, u32[]{:S(2)}) copy-start(bf16[4,384,384]{2,1,0:T(8,128)(2,1)} %get-tuple-element.858) | copy-start | bytes 3538948 | tf_op jit(solution)/shard_map/while
  137.5 3.6 %copy-start.1 = (bf16[4,384,384]{2,1,0:T(8,128)(2,1)S(1)}, bf16[4,384,384]{2,1,0:T(8,128)(2,1)}, u32[]{:S(2)}) copy-start(bf16[4,384,384]{2,1,0:T(8,128)(2,1)} %get-tuple-element.858) | copy-start | bytes 3538948 | tf_op jit(solution)/shard_map/while
  155.7 3.6 %copy-start.1 = (bf16[4,384,384]{2,1,0:T(8,128)(2,1)S(1)}, bf16[4,384,384]{2,1,0:T(8,128)(2,1)}, u32[]{:S(2)}) copy-start(bf16[4,384,384]{2,1,0:T(8,128)(2,1)} %get-tuple-element.858) | copy-start | bytes 3538948 | tf_op jit(solution)/shard_map/while
  173.9 3.6 %copy-start.1 = (bf16[4,384,384]{2,1,0:T(8,128)(2,1)S(1)}, bf16[4,384,384]{2,1,0:T(8,128)(2,1)}, u32[]{:S(2)}) copy-start(bf16[4,384,384]{2,1,0:T(8,128)(2,1)} %get-tuple-element.858) | copy-start | bytes 3538948 | tf_op jit(solution)/shard_map/while
  178.7 2.4 copy-start.2
  178.7 2.4 copy-start.7
  184.3 23.6 %all-to-all-start = ((f32[384,8,128]{2,1,0:T(8,128)}), f32[384,8,128]{2,1,0:T(8,128)S(1)}, u32[]{:S(2)}, u32[]{:S(2)}) async-start(f32[384,8,128]{2,1,0:T(8,128)} %copy.57), calls=%async_computation | async-start | bytes 3145728 | tf_op jit(solution)/shard_map/all_to_all | solution.py:168
  215.0 5.7 %copy-start.5 = (f32[8,8,8,64]{3,2,1,0:T(8,128)S(1)}, f32[8,8,8,64]{3,2,1,0:T(8,128)}, u32[]{:S(2)}) copy-start(f32[8,8,8,64]{3,2,1,0:T(8,128)} %custom-call.8) | copy-start | bytes 393220
  216.1 100.1 %all-to-all-start.1 = ((f32[2,64,96,8]{2,3,0,1:T(8,128)}), f32[2,64,96,8]{2,3,0,1:T(8,128)S(1)}, u32[]{:S(2)}, u32[]{:S(2)}) async-start(f32[2,64,96,8]{2,3,0,1:T(8,128)} %copy.59), calls=%async_computation.1 | async-start | bytes 1048576 | tf_op jit(solution)/shard_map/all_to_all | solution.py:175
  318.6 19.7 %all-to-all-start.2 = ((f32[2,8,96,64]{2,0,1,3:T(2,128)}), f32[2,8,96,64]{2,0,1,3:T(2,128)S(1)}, u32[]{:S(2)}, u32[]{:S(2)}) async-start(f32[2,8,96,64]{2,0,1,3:T(2,128)} %copy.65), calls=%async_computation.2 | async-start | bytes 1048576 | tf_op jit(solution)/shard_map/all_to_all | solution.py:179
  340.8 6.6 %collective-permute-start.4 = (bf16[96,8,128]{2,1,0:T(8,128)(2,1)S(1)}, bf16[96,8,128]{2,1,0:T(8,128)(2,1)S(1)}, u32[]{:S(2)}, u32[]{:S(2)}) collective-permute-start(bf16[96,8,128]{2,1,0:T(8,128)(2,1)S(1)} %get-tuple-element.575), channel_id=1, source_target_pairs={{0,1},{1,2},{2,3},{3,0},{4,5},{5,6},{6,7},{7,4},{8,9},{9,10},{10,1... | collective-permute-start | bytes 589832 | tf_op jit(solution)/shard_map/ppermute | solution.py:195
  340.8 7.8 %collective-permute-start.5 = (bf16[96,8,128]{2,1,0:T(8,128)(2,1)S(1)}, bf16[96,8,128]{2,1,0:T(8,128)(2,1)S(1)}, u32[]{:S(2)}, u32[]{:S(2)}) collective-permute-start(bf16[96,8,128]{2,1,0:T(8,128)(2,1)S(1)} %get-tuple-element.574), channel_id=1, source_target_pairs={{0,2},{1,3},{2,0},{3,1},{4,6},{5,7},{6,4},{7,5},{8,10},{9,11},{10,... | collective-permute-start | bytes 589832 | tf_op jit(solution)/shard_map/ppermute | solution.py:195
  341.9 8.9 %collective-permute-start.6 = (bf16[96,8,128]{2,1,0:T(8,128)(2,1)S(1)}, bf16[96,8,128]{2,1,0:T(8,128)(2,1)S(1)}, u32[]{:S(2)}, u32[]{:S(2)}) collective-permute-start(bf16[96,8,128]{2,1,0:T(8,128)(2,1)S(1)} %get-tuple-element.573), channel_id=1, source_target_pairs={{0,3},{1,0},{2,1},{3,2},{4,7},{5,4},{6,5},{7,6},{8,11},{9,8},{10,9... | collective-permute-start | bytes 589832 | tf_op jit(solution)/shard_map/ppermute | solution.py:195
